TPU v7x, 32 devices: a whole 2x2x4 slice. The times are simulated.
32 devices in a mesh: row: 4 (over y, x), col: 8 (over z, core).
Axes of the slice: x: 2, y: 2, z: 4, core: 2. Of those that a mesh axis runs over, the one named last changes fastest.
Arguments:
- eigvecs: float32 [4096, 4096], P('row', 'col'), may hold values from -6 to 6
- house_one: float32 [4096, 128], P('row', 'col'), may hold values from -0.09375 to 0.09375
- house_two: float32 [4096, 128], P('row', 'col'), may hold values from -0.09375 to 0.09375
- tile_map: int32 [32], replicated, may hold values from 0 to 31, each once
- select: int32 [256], replicated, may hold values from 0 to 4095, as said below
- ritz_basis: bfloat16 [32768, 4096], P(('row', 'col')), may hold values from -0.09375 to 0.09375
Outputs:
- back_vectors: float32 [4096, 4096], P('row', 'col')
- mode_shapes: bfloat16 [32768, 256], P(('row', 'col'))
Inputs may be any that keep to these rules, and one draw needn't show every extreme that they name: `select`: the 256 indices are distinct and include 0 and 4095. `tile_map`: each global tile row appears once.
All inputs are finite; a program needn't handle non-finite values.
Results may differ from a plain program's by a relative error of at most 0.0049.
Values may be sent and summed in bfloat16 or wider, within the bound.
No kernel may reach another device: no remote copies, remote signals or barrier semaphores. Data moves between devices by JAX's collectives and lax.ppermute only.
A program may use at most 64 MiB of HBM per device.

v0:
```python
import jax
import jax.numpy as jnp
from jax import lax
from jax.sharding import PartitionSpec as P

TILE = 128


def precise(left, right):
    return jnp.dot(left, right, precision=lax.Precision.HIGHEST, preferred_element_type=jnp.float32)


def compact(gram):
    width = gram.shape[0]
    scales = 0.5 * jnp.diag(gram)
    strict = jnp.triu(gram, 1) / scales[:, None]
    identity = jnp.eye(width, dtype=gram.dtype)
    power = -strict
    total = identity + power
    for level in range((width - 1).bit_length() - 1):
        power = precise(power, power)
        total = precise(total, identity + power)
    return total / scales[None, :]


def expand_panel(panel, tile_map, ritz_basis):
    tile_count = tile_map.shape[0]
    tiles = panel.reshape(tile_count, TILE, panel.shape[1])
    places = jnp.arange(tile_count, dtype=jnp.int32)
    mover = (places[:, None] == tile_map[None, :]).astype(jnp.bfloat16)
    ordered = jnp.einsum("gs,sip->gip", mover, tiles, preferred_element_type=jnp.float32)
    ordered = ordered.astype(jnp.bfloat16).reshape(panel.shape[0], panel.shape[1])
    return jnp.dot(ritz_basis, ordered, preferred_element_type=jnp.float32)


def per_device(eigvecs, house_one, house_two, tile_map, select, ritz_basis):
    vec_one, vec_two = (
        lax.all_gather(house_one, "col", axis=1, tiled=True),
        lax.all_gather(house_two, "col", axis=1, tiled=True),
    )

    def apply_block(field, vectors):
        projected, gram = lax.psum((precise(vectors.T, field), precise(vectors.T, vectors)), "row")
        return field - precise(vectors, precise(compact(gram), projected))

    section = apply_block(eigvecs, vec_two)
    back_vectors = apply_block(section, vec_one)
    local_cols = eigvecs.shape[1]
    col_ids = lax.axis_index("col") * local_cols + jnp.arange(local_cols, dtype=jnp.int32)
    chooser = (col_ids[:, None] == select[None, :]).astype(jnp.float32)
    picked = precise(back_vectors, chooser)
    rows_part = lax.psum(picked.astype(jnp.bfloat16), "col")
    panel = lax.all_gather(rows_part, "row", axis=0, tiled=True)
    modes = expand_panel(panel, tile_map, ritz_basis)
    return (back_vectors, modes.astype(jnp.bfloat16))


def solution(mesh):
    return jax.shard_map(
        per_device,
        mesh=mesh,
        in_specs=(
            P("row", "col"),
            P("row", "col"),
            P("row", "col"),
            P(),
            P(),
            P(("row", "col"), None),
        ),
        out_specs=(P("row", "col"), P(("row", "col"), None)),
        check_vma=False,
    )
```

profile of v0, /device:TPU:0, one launch (start us, length us, event | category | flops | bytes accessed | tf_op | source)
XLA Modules:
  0.0 253.1 jit_solution(4916615402586915821)
XLA Ops:
  7.2 0.0 all-reduce.10.cloned.1.call-start
  7.2 16.8 %all_gather.9 = f32[1024,128]{0,1:T(8,128)S(1)} all-gather(f32[1024,16]{0,1:T(8,128)} %param.8), channel_id=1, replica_groups=mesh['row'=4,'col'=8] {'col'}, dimensions={1}, use_global_device_ids=true | all-gather | bytes 589824 | tf_op jit(solution)/shard_map/all_gather | solution.py:39
  24.0 1.2 fusion.24
  25.2 3.6 %fusion.29 = f32[128,512]{1,0:T(8,128)} fusion(f32[1024,128]{0,1:T(8,128)S(1)} %all_gather.9, f32[1024,512]{1,0:T(8,128)} %param.6), kind=kOutput, calls=%fused_computation.58 | convolution fusion | flops 805306368 | bytes 2883584 | tf_op jit(solution)/shard_map/dot_general | solution.py:10
  28.8 0.0 all-reduce.10.cloned.1.call-update
  28.8 0.0 copy-start.4
  28.8 0.0 all-reduce.8.cloned.1.call-start
  28.9 0.0 copy-done.1
  28.9 1.8 copy.12
  30.7 14.7 %all_gather.10 = f32[1024,128]{0,1:T(8,128)S(1)} all-gather(f32[1024,16]{0,1:T(8,128)S(1)} %copy-done.4), channel_id=1, replica_groups=mesh['row'=4,'col'=8] {'col'}, dimensions={1}, use_global_device_ids=true | all-gather | bytes 589824 | tf_op jit(solution)/shard_map/all_gather | solution.py:38
  45.4 1.2 fusion.31
  46.7 27.0 %all-reduce.10.cloned.1.call-done = (f32[128,128]{1,0:T(8,128)}, f32[128,512]{1,0:T(8,128)}) async-done(((f32[128,128]{1,0:T(8,128)}, f32[128,512]{1,0:T(8,128)}), (f32[128,128]{1,0:T(8,128)}, f32[128,512]{1,0:T(8,128)})) %all-reduce.10.cloned.1.call-update) | async-done | bytes 327696 | tf_op jit(solution)/shard_map/psum | solution.py:43
  73.7 2.0 gather_fusion
  75.7 1.2 fusion.22
  76.9 1.1 fusion.9
  78.0 0.2 fusion.25
  78.2 0.2 fusion.26
  78.4 0.2 fusion.10
  78.6 0.2 fusion.27
  78.8 0.2 fusion.11
  79.1 0.2 fusion.28
  79.3 0.2 fusion.12
  79.5 0.2 convolution_add_fusion.1
  79.7 0.2 fusion.13
  79.9 0.2 convolution_divide_fusion.1
  80.1 0.0 copy-done.3
  80.1 0.4 fusion.30
  80.5 3.5 %bitcast_subtract_fusion.1 = f32[1024,512]{0,1:T(8,128)S(1)} fusion(f32[1024,512]{0,1:T(8,128)} %copy.12, f32[128,512]{1,0:T(8,128)S(1)} %fusion.30, f32[1024,128]{0,1:T(8,128)S(1)} %all_gather.9), kind=kOutput, calls=%fused_computation.3 | convolution fusion | flops 805830656 | bytes 4980736 | tf_op jit(solution)/shard_map/dot_general | solution.py:10
  84.0 2.5 convolution_bitcast_fusion
  86.5 0.0 all-reduce.8.cloned.1.call-update
  86.5 0.2 all-reduce.6.cloned.1.call-start
  86.8 43.6 %all-reduce.8.cloned.1.call-done = (f32[128,128]{1,0:T(8,128)}, f32[128,512]{0,1:T(8,128)}) async-done(((f32[128,128]{1,0:T(8,128)}, f32[128,512]{0,1:T(8,128)}), (f32[128,128]{1,0:T(8,128)}, f32[128,512]{0,1:T(8,128)})) %all-reduce.8.cloned.1.call-update) | async-done | bytes 327696 | tf_op jit(solution)/shard_map/psum | solution.py:43
  130.3 2.0 gather_fusion.1
  132.3 1.2 fusion.23
  133.5 1.1 fusion.14
  134.6 0.2 fusion.32
  134.8 0.2 fusion.33
  135.1 0.2 fusion.15
  135.3 0.2 fusion.34
  135.5 0.2 fusion.16
  135.7 0.2 fusion.35
  135.9 0.2 fusion.17
  136.1 0.2 convolution_add_fusion
  136.3 0.2 fusion.18
  136.6 0.2 convolution_divide_fusion
  136.8 0.0 copy-done.2
  136.8 0.4 fusion.36
  137.2 0.0 copy-start.5
  137.2 1.9 bitcast_subtract_fusion
  139.1 0.0 copy-start
  139.1 1.3 copy-done
  140.4 2.7 %convolution_convert_fusion.1 = bf16[1024,256]{1,0:T(8,128)(2,1)} fusion(f32[1024,512]{0,1:T(8,128)S(1)} %bitcast_subtract_fusion, s32[256]{0:T(256)S(1)} %copy-done.5, s32[512]{0:T(512)S(1)} %iota_add_fusion), kind=kOutput, calls=%fused_computation.8 | convolution fusion | flops 1611005952 | bytes 2624512 | tf_op jit(solution)/shard_map/dot_general | solution.py:10
  143.1 0.0 all-reduce.6.cloned.1.call-update
  143.1 0.0 all-gather.2.cloned.1.call-start
  143.2 56.2 %all-reduce.6.cloned.1.call-done = bf16[1024,256]{1,0:T(8,128)(2,1)} async-done(((bf16[1024,256]{1,0:T(8,128)(2,1)}), bf16[1024,256]{1,0:T(8,128)(2,1)}) %all-reduce.6.cloned.1.call-update) | async-done | bytes 524304 | tf_op jit(solution)/shard_map/psum | solution.py:52
  199.4 0.0 all-gather.2.cloned.1.call-update
  199.5 0.0 copy-start.6
  199.5 2.9 %copy.15 = f32[1024,512]{1,0:T(8,128)} copy(f32[1024,512]{0,1:T(8,128)} %copy-done) | data formatting | bytes 4194304
  202.4 33.2 %all-gather.2.cloned.1.call-done = bf16[4096,256]{1,0:T(8,128)(2,1)} async-done(((bf16[1024,256]{1,0:T(8,128)(2,1)}), bf16[4096,256]{1,0:T(8,128)(2,1)}) %all-gather.2.cloned.1.call-update) | async-done | bytes 2097168 | tf_op jit(solution)/shard_map/all_gather | solution.py:53
  235.6 0.0 copy-done.6
  235.6 3.0 %fusion.2 = bf16[32,128,256]{2,0,1:T(8,128)(2,1)S(1)} fusion(bf16[32,128,256]{2,1,0:T(8,128)(2,1)} %bitcast.66, s32[32]{0:T(128)S(1)} %copy-done.6), kind=kOutput, calls=%fused_computation.6 | convolution fusion | flops 68158464 | bytes 4194432 | tf_op jit(solution)/shard_map/gs,sip->gip/dot_general | solution.py:31
  238.6 1.2 copy.14
  239.7 5.8 %fusion.5 = bf16[1024,256]{0,1:T(8,128)(2,1)S(1)} fusion(bf16[4096,256]{1,0:T(8,128)(2,1)S(1)} %bitcast.67, bf16[1024,4096]{1,0:T(8,128)(2,1)} %param.11), kind=kOutput, calls=%fused_computation.9 | convolution fusion | flops 2147745792 | bytes 11010048 | tf_op jit(solution)/shard_map/dot_general | solution.py:33
  245.5 1.0 copy.16
  (9 shorter events, 0.0 us)
Async XLA Ops:
  7.2 66.5 %all-reduce.10.cloned.1.call-start = ((), (), s32[]{:S(2)}) async-start(), calls=%async_computation.3 | async-start | bytes 655360 | tf_op jit(solution)/shard_map/psum | solution.py:43
  24.0 4.9 %copy-start.1 = (f32[1024,512]{1,0:T(8,128)S(1)}, f32[1024,512]{1,0:T(8,128)}, u32[]{:S(2)}) copy-start(f32[1024,512]{1,0:T(8,128)} %param.6) | copy-start | bytes 6291460
  28.8 1.9 copy-start.4
  28.8 101.5 %all-reduce.8.cloned.1.call-start = ((), (), s32[]{:S(2)}) async-start(), calls=%async_computation.2 | async-start | bytes 655360 | tf_op jit(solution)/shard_map/psum | solution.py:43
  73.7 6.4 %copy-start.3 = (f32[128,512]{1,0:T(8,128)S(1)}, f32[128,512]{1,0:T(8,128)}, u32[]{:S(2)}) copy-start(f32[128,512]{1,0:T(8,128)} %get-tuple-element.9) | copy-start | bytes 786436
  86.5 112.9 %all-reduce.6.cloned.1.call-start = ((), (), s32[]{:S(2)}) async-start(), calls=%async_computation | async-start | bytes 1048576 | tf_op jit(solution)/shard_map/psum | solution.py:52
  130.3 6.4 %copy-start.2 = (f32[128,512]{0,1:T(8,128)S(1)}, f32[128,512]{0,1:T(8,128)}, u32[]{:S(2)}) copy-start(f32[128,512]{0,1:T(8,128)} %get-tuple-element.7) | copy-start | bytes 786436
  137.2 3.2 %copy-start.5 = (s32[256]{0:T(256)S(1)}, s32[256]{0:T(256)}, u32[]{:S(2)}) copy-start(s32[256]{0:T(256)} %param.10) | copy-start | bytes 3076
  139.1 1.3 copy-start
  143.1 92.5 %all-gather.2.cloned.1.call-start = ((), (), s32[]{:S(2)}) async-start(), calls=%async_computation.1 | async-start | bytes 2621440 | tf_op jit(solution)/shard_map/all_gather | solution.py:53
  199.5 36.1 %copy-start.6 = (s32[32]{0:T(128)S(1)}, s32[32]{0:T(128)}, u32[]{:S(2)}) copy-start(s32[32]{0:T(128)} %param.9) | copy-start | bytes 388
Sparse Core Ops, SparseCore 0:
  29.0 44.6 all-reduce.9
  86.7 43.6 all-reduce.7
  143.3 56.1 all-reduce.5
  201.3 34.2 all-gather.1
where the time goes:
time: 254 us; the launch traced here: 253 us
  waiting for transfers between devices  160 us (63%)
  matrix products  34.8 us (14%)
  blocking collectives  31.5 us (12%)
  between operations  14.1 us (6%)
  local copies, waits for them, and re-layouts  12.2 us (5%)
    psum x2, waiting for transfers between devices, apply_block(): lax.psum((precise(vectors.T, field), precise(vectors.T, vectors)), 'row')  70.6 us
    psum x1, waiting for transfers between devices, per_device(): rows_part = lax.psum(picked.astype(jnp.bfloat16), 'col')  56.2 us
    all_gather x1, waiting for transfers between devices, per_device(): panel = lax.all_gather(rows_part, 'row', axis=0, tiled=True)  33.2 us
    dot_general x33, matrix products, precise(): jnp.dot(left, right, precision=lax.Precision.HIGHEST, preferred_element_t...  26.1 us
    all_gather x1, blocking collectives, per_device(): lax.all_gather(house_two, 'col', axis=1, tiled=True)  16.8 us
    all_gather x1, blocking collectives, per_device(): lax.all_gather(house_one, 'col', axis=1, tiled=True)  14.7 us
    unnamed x17, local copies, waits for them, and re-layouts  7.04 us
    dot_general x1, matrix products, expand_panel(): return jnp.dot(ritz_basis, ordered, preferred_element_type=jnp.float32)  5.77 us
  transfers between devices with their start and end apart: 4, of which 4 were waited for; matrix products, arithmetic and copies ran while one was open for 2% of the time, Pallas kernels for 0%

commit v1 on v0

--- a/solution.py
+++ b/solution.py
@@ -49,7 +49,9 @@
     col_ids = lax.axis_index("col") * local_cols + jnp.arange(local_cols, dtype=jnp.int32)
     chooser = (col_ids[:, None] == select[None, :]).astype(jnp.float32)
     picked = precise(back_vectors, chooser)
-    rows_part = lax.psum(picked.astype(jnp.bfloat16), "col")
+    own = picked.astype(jnp.bfloat16)
+    shards = lax.all_gather(own, "col")
+    rows_part = jnp.sum(shards, axis=0)
     panel = lax.all_gather(rows_part, "row", axis=0, tiled=True)
     modes = expand_panel(panel, tile_map, ritz_basis)
     return (back_vectors, modes.astype(jnp.bfloat16))

time: 254 us -> 246 us (0.969)
  waiting for transfers between devices: 160 us -> 150 us
  other arithmetic: 0.02 us -> 3.86 us
    psum x1 -> x0, waiting for transfers between devices: 56.2 us -> none  [per_device(): rows_part = lax.psum(picked.astype(jnp.bfloat16), 'col')]
    all_gather x0 -> x1, waiting for transfers between devices: none -> 47 us  [per_device(): shards = lax.all_gather(own, 'col')]
    reduce_sum x0 -> x1, other arithmetic: none -> 3.83 us  [per_device(): rows_part = jnp.sum(shards, axis=0)]
    unnamed x17 -> x19, local copies, waits for them, and re-layouts: 7.04 us -> 5.98 us
where the time goes in v1:
time: 246 us
  waiting for transfers between devices  150 us (61%)
  matrix products  34.8 us (14%)
  blocking collectives  31.5 us (13%)
  between operations  14.1 us (6%)
  local copies, waits for them, and re-layouts  11.1 us (5%)
  other arithmetic  3.86 us (2%)
    psum x2, waiting for transfers between devices, apply_block(): lax.psum((precise(vectors.T, field), precise(vectors.T, vectors)), 'row')  70.6 us
    all_gather x1, waiting for transfers between devices, per_device(): shards = lax.all_gather(own, 'col')  47 us
    all_gather x1, waiting for transfers between devices, per_device(): panel = lax.all_gather(rows_part, 'row', axis=0, tiled=True)  32.3 us
    dot_general x33, matrix products, precise(): jnp.dot(left, right, precision=lax.Precision.HIGHEST, preferred_element_t...  26 us
    all_gather x1, blocking collectives, per_device(): lax.all_gather(house_two, 'col', axis=1, tiled=True)  16.8 us
    all_gather x1, blocking collectives, per_device(): lax.all_gather(house_one, 'col', axis=1, tiled=True)  14.7 us
    unnamed x19, local copies, waits for them, and re-layouts  5.98 us
    dot_general x1, matrix products, expand_panel(): return jnp.dot(ritz_basis, ordered, preferred_element_type=jnp.float32)  5.77 us
  transfers between devices with their start and end apart: 4, of which 4 were waited for; matrix products, arithmetic and copies ran while one was open for 2% of the time, Pallas kernels for 0%

profile of v1, /device:TPU:0, one launch (start us, length us, event | category | flops | bytes accessed | tf_op | source)
XLA Modules:
  0.0 245.9 jit_solution(17700642528129598380)
XLA Ops:
  7.2 0.0 all-reduce.7.cloned.1.call-start
  7.2 16.8 %all_gather.15 = f32[1024,128]{0,1:T(8,128)S(1)} all-gather(f32[1024,16]{0,1:T(8,128)} %param.8), channel_id=1, replica_groups=mesh['row'=4,'col'=8] {'col'}, dimensions={1}, use_global_device_ids=true | all-gather | bytes 589824 | tf_op jit(solution)/shard_map/all_gather | solution.py:39
  24.0 1.2 fusion.24
  25.2 3.6 %fusion.29 = f32[128,512]{1,0:T(8,128)} fusion(f32[1024,128]{0,1:T(8,128)S(1)} %all_gather.15, f32[1024,512]{1,0:T(8,128)} %param.6), kind=kOutput, calls=%fused_computation.58 | convolution fusion | flops 805306368 | bytes 2883584 | tf_op jit(solution)/shard_map/dot_general | solution.py:10
  28.8 0.0 all-reduce.7.cloned.1.call-update
  28.8 0.0 copy-start.5
  28.8 0.0 all-reduce.5.cloned.1.call-start
  28.9 0.0 copy-done.2
  28.9 1.8 copy.11
  30.7 0.0 copy-done.5
  30.7 14.7 %all_gather.16 = f32[1024,128]{0,1:T(8,128)S(1)} all-gather(f32[1024,16]{0,1:T(8,128)S(1)} %copy-done.5), channel_id=1, replica_groups=mesh['row'=4,'col'=8] {'col'}, dimensions={1}, use_global_device_ids=true | all-gather | bytes 589824 | tf_op jit(solution)/shard_map/all_gather | solution.py:38
  45.4 1.2 fusion.31
  46.6 27.0 %all-reduce.7.cloned.1.call-done = (f32[128,128]{1,0:T(8,128)}, f32[128,512]{1,0:T(8,128)}) async-done(((f32[128,128]{1,0:T(8,128)}, f32[128,512]{1,0:T(8,128)}), (f32[128,128]{1,0:T(8,128)}, f32[128,512]{1,0:T(8,128)})) %all-reduce.7.cloned.1.call-update) | async-done | bytes 327696 | tf_op jit(solution)/shard_map/psum | solution.py:43
  73.7 2.0 gather_fusion
  75.7 1.2 fusion.22
  76.9 1.1 fusion.9
  78.0 0.2 fusion.25
  78.2 0.2 fusion.26
  78.4 0.2 fusion.10
  78.6 0.2 fusion.27
  78.8 0.2 fusion.11
  79.0 0.2 fusion.28
  79.3 0.2 fusion.12
  79.5 0.2 convolution_add_fusion.1
  79.7 0.2 fusion.13
  79.9 0.2 convolution_divide_fusion.1
  80.1 0.4 fusion.30
  80.5 3.5 %bitcast_subtract_fusion.1 = f32[1024,512]{0,1:T(8,128)S(1)} fusion(f32[1024,512]{0,1:T(8,128)} %copy.11, f32[128,512]{1,0:T(8,128)S(1)} %fusion.30, f32[1024,128]{0,1:T(8,128)S(1)} %all_gather.15), kind=kOutput, calls=%fused_computation.3 | convolution fusion | flops 805830656 | bytes 4980736 | tf_op jit(solution)/shard_map/dot_general | solution.py:10
  84.0 2.5 %convolution_bitcast_fusion = f32[128,512]{0,1:T(8,128)} fusion(f32[1024,512]{0,1:T(8,128)S(1)} %bitcast_subtract_fusion.1, f32[1024,128]{0,1:T(8,128)S(1)} %all_gather.16), kind=kOutput, calls=%fused_computation.10 | convolution fusion | flops 805306368 | bytes 2883584 | tf_op jit(solution)/shard_map/dot_general | solution.py:10
  86.5 0.0 all-reduce.5.cloned.1.call-update
  86.5 0.2 all-gather.6.cloned.1.call-start
  86.8 43.6 %all-reduce.5.cloned.1.call-done = (f32[128,128]{1,0:T(8,128)}, f32[128,512]{0,1:T(8,128)}) async-done(((f32[128,128]{1,0:T(8,128)}, f32[128,512]{0,1:T(8,128)}), (f32[128,128]{1,0:T(8,128)}, f32[128,512]{0,1:T(8,128)})) %all-reduce.5.cloned.1.call-update) | async-done | bytes 327696 | tf_op jit(solution)/shard_map/psum | solution.py:43
  130.3 2.0 gather_fusion.1
  132.3 1.2 fusion.23
  133.5 1.1 fusion.14
  134.6 0.2 fusion.32
  134.8 0.2 fusion.33
  135.1 0.2 fusion.15
  135.3 0.2 fusion.34
  135.5 0.2 fusion.16
  135.7 0.2 fusion.35
  135.9 0.2 fusion.17
  136.1 0.2 convolution_add_fusion
  136.3 0.2 fusion.18
  136.5 0.2 convolution_divide_fusion
  136.8 0.0 copy-done.3
  136.8 0.4 fusion.36
  137.1 0.0 copy-start.6
  137.2 1.9 bitcast_subtract_fusion
  139.1 0.0 copy-start
  139.1 1.3 copy-done
  140.4 2.7 %convolution_convert_fusion.1 = bf16[1024,256]{1,0:T(8,128)(2,1)} fusion(f32[1024,512]{0,1:T(8,128)S(1)} %bitcast_subtract_fusion, s32[256]{0:T(256)S(1)} %copy-done.6, s32[512]{0:T(512)S(1)} %iota_add_fusion), kind=kOutput, calls=%fused_computation.8 | convolution fusion | flops 1611005952 | bytes 2624512 | tf_op jit(solution)/shard_map/dot_general | solution.py:10
  143.1 0.0 all-gather.6.cloned.1.call-update
  143.1 0.3 all-gather.4.cloned.1.call-start
  143.4 47.0 %all-gather.6.cloned.1.call-done = bf16[8192,256]{1,0:T(8,128)(2,1)} async-done(((bf16[1024,256]{1,0:T(8,128)(2,1)}), bf16[8192,256]{1,0:T(8,128)(2,1)}) %all-gather.6.cloned.1.call-update) | async-done | bytes 4194320 | tf_op jit(solution)/shard_map/all_gather | solution.py:53
  190.4 3.8 %reduce_sum.12 = bf16[1024,256]{1,0:T(8,128)(2,1)} reduce(bf16[8,1024,256]{2,1,0:T(8,128)(2,1)} %bitcast.67, bf16[]{:T(256)} %constant.23.clone.1), dimensions={0}, to_apply=%region_4.5 | reduce | flops 1835008 | bytes 4718594 | tf_op jit(solution)/shard_map/reduce_sum | solution.py:54
  194.3 0.0 all-gather.4.cloned.1.call-update
  194.3 0.0 copy-start.7
  194.3 1.8 copy.14
  196.1 32.3 %all-gather.4.cloned.1.call-done = bf16[4096,256]{1,0:T(8,128)(2,1)} async-done(((bf16[1024,256]{1,0:T(8,128)(2,1)}), bf16[4096,256]{1,0:T(8,128)(2,1)}) %all-gather.4.cloned.1.call-update) | async-done | bytes 2097168 | tf_op jit(solution)/shard_map/all_gather | solution.py:55
  228.5 3.0 %fusion.2 = bf16[32,128,256]{2,0,1:T(8,128)(2,1)S(1)} fusion(bf16[32,128,256]{2,1,0:T(8,128)(2,1)} %bitcast.68, s32[32]{0:T(128)S(1)} %copy-done.7), kind=kOutput, calls=%fused_computation.6 | convolution fusion | flops 68158464 | bytes 4194432 | tf_op jit(solution)/shard_map/gs,sip->gip/dot_general | solution.py:31
  231.4 1.2 copy.13
  232.6 5.8 %fusion.5 = bf16[1024,256]{0,1:T(8,128)(2,1)S(1)} fusion(bf16[4096,256]{1,0:T(8,128)(2,1)S(1)} %bitcast.69, bf16[1024,4096]{1,0:T(8,128)(2,1)} %param.11), kind=kOutput, calls=%fused_computation.9 | convolution fusion | flops 2147745792 | bytes 11010048 | tf_op jit(solution)/shard_map/dot_general | solution.py:33
  238.4 1.0 copy.15
  (12 shorter events, 0.0 us)
Async XLA Ops:
  7.2 66.5 %all-reduce.7.cloned.1.call-start = ((), (), s32[]{:S(2)}) async-start(), calls=%async_computation.3 | async-start | bytes 655360 | tf_op jit(solution)/shard_map/psum | solution.py:43
  24.0 4.9 %copy-start.2 = (f32[1024,512]{1,0:T(8,128)S(1)}, f32[1024,512]{1,0:T(8,128)}, u32[]{:S(2)}) copy-start(f32[1024,512]{1,0:T(8,128)} %param.6) | copy-start | bytes 6291460
  28.8 1.9 copy-start.5
  28.8 101.5 %all-reduce.5.cloned.1.call-start = ((), (), s32[]{:S(2)}) async-start(), calls=%async_computation.2 | async-start | bytes 655360 | tf_op jit(solution)/shard_map/psum | solution.py:43
  73.7 6.4 %copy-start.4 = (f32[128,512]{1,0:T(8,128)S(1)}, f32[128,512]{1,0:T(8,128)}, u32[]{:S(2)}) copy-start(f32[128,512]{1,0:T(8,128)} %get-tuple-element.9) | copy-start | bytes 786436
  86.5 103.9 %all-gather.6.cloned.1.call-start = ((), (), s32[]{:S(2)}) async-start(), calls=%async_computation.1 | async-start | bytes 4718592 | tf_op jit(solution)/shard_map/all_gather | solution.py:53
  130.3 6.4 %copy-start.3 = (f32[128,512]{0,1:T(8,128)S(1)}, f32[128,512]{0,1:T(8,128)}, u32[]{:S(2)}) copy-start(f32[128,512]{0,1:T(8,128)} %get-tuple-element.7) | copy-start | bytes 786436
  137.1 3.2 %copy-start.6 = (s32[256]{0:T(256)S(1)}, s32[256]{0:T(256)}, u32[]{:S(2)}) copy-start(s32[256]{0:T(256)} %param.10) | copy-start | bytes 3076
  139.1 1.3 copy-start
  143.1 85.3 %all-gather.4.cloned.1.call-start = ((), (), s32[]{:S(2)}) async-start(), calls=%async_computation | async-start | bytes 2621440 | tf_op jit(solution)/shard_map/all_gather | solution.py:55
  190.4 3.9 %copy-start.1 = (f32[1024,512]{0,1:T(8,128)S(1)}, f32[1024,512]{0,1:T(8,128)}, u32[]{:S(2)}) copy-start(f32[1024,512]{0,1:T(8,128)} %copy-done) | copy-start | bytes 6291460
  194.3 34.2 %copy-start.7 = (s32[32]{0:T(128)S(1)}, s32[32]{0:T(128)}, u32[]{:S(2)}) copy-start(s32[32]{0:T(128)} %param.9) | copy-start | bytes 388
Sparse Core Ops, SparseCore 0:
  28.9 44.6 all-reduce.6
  86.6 43.6 all-reduce.4
  143.3 47.1 all-gather.5
  194.4 34.0 all-gather.3
